TPU v7x, 256 devices: a whole 4x4x8 slice. The times are simulated.
256 devices in a mesh: section: 8 (over y, x_hi), ctx: 32 (over x_lo, z, core).
Axes of the slice: x: 4 (x_hi: 2, x_lo: 2; x = x_hi * 2 + x_lo), y: 4, z: 8, core: 2. Of those that a mesh axis runs over, the one named last changes fastest.
Arguments:
- queries: bfloat16 [8, 12288, 40, 128], P('section', 'ctx'), may hold values from -60 to 60
- keys_values: bfloat16 [12288, 2, 40, 128], P('ctx', None, 'section'), may hold values from -6 to 6
- positions: int32 [12288], P('ctx'), may hold values from 0 to 1533, as said below
- documents: int32 [12288], P('ctx'), may hold values from 0 to 12287, as said below
Outputs:
- attended: bfloat16 [8, 12288, 40, 128], P('section', 'ctx')
Inputs may be any that keep to these rules, and one draw needn't show every extreme that they name: `documents`: Non-decreasing along the sequence; each document is a run of 1 to 384 tokens sharing one id, one document has exactly 384 tokens, and the last document's id is 12287. `positions`: within a document the ids rise by 1 to 3 from each token to the next; a document's first id is 0 to 384.
All inputs are finite; a program needn't handle non-finite values.
Results may differ from a plain program's by a relative error of at most 0.01.
Values may be sent and summed in bfloat16 or wider, within the bound.
A program may use at most 128 MiB of HBM per device.

v0:
```python
import jax
import jax.numpy as jnp
from jax import lax
from jax.sharding import PartitionSpec as P


def shifted(block, axis, distance):
    devices = range(lax.axis_size(axis))
    route = [(i - distance, i) for i in devices if i - distance in devices]
    return lax.ppermute(block, axis, route)


def rotate(values, token_positions):
    half_dim = values.shape[-1] // 2
    exponent = jnp.arange(half_dim, dtype=jnp.float32) * (2.0 / values.shape[-1])
    inverse = jnp.power(jnp.float32(10000.0), -exponent)
    angles = token_positions.astype(jnp.float32)[:, None] * inverse[None, :]
    cosine = jnp.cos(angles)[:, None, :]
    sine = jnp.sin(angles)[:, None, :]
    widened = values.astype(jnp.float32)
    lower = widened[..., :half_dim]
    upper = widened[..., half_dim:]
    joined = jnp.concatenate(
        [lower * cosine - upper * sine, upper * cosine + lower * sine], axis=-1
    )
    return joined.astype(jnp.bfloat16)


def attend(rotated, piece, key_docs, query_docs):
    query_rows = query_docs.shape[0]
    key_rows = key_docs.shape[0]
    head_count = piece.shape[2]
    head_dim = piece.shape[3]
    factor = max((option for option in range(1, 9) if head_count % option == 0))
    groups = head_count // factor

    def split_heads(values, length):
        return jnp.moveaxis(values.reshape(length, groups, factor, head_dim), 1, 0)

    allowed = jnp.logical_and(
        key_docs[None, :] == query_docs[:, None],
        jnp.arange(key_rows)[None, :] <= jnp.arange(query_rows)[:, None] + (key_rows - query_rows),
    )
    scale = head_dim ** (-0.5)

    def one_group(operands):
        query_part, key_part, value_part = operands
        scores = (
            jnp.einsum("qhd,khd->hqk", query_part, key_part, preferred_element_type=jnp.float32)
            * scale
        )
        scores = jnp.where(allowed[None], scores, -1e30)
        largest = jnp.max(scores, axis=-1, keepdims=True)
        weights = jnp.exp(scores - largest)
        probs = (weights / jnp.sum(weights, axis=-1, keepdims=True)).astype(jnp.bfloat16)
        mixed = jnp.einsum("hqk,khd->qhd", probs, value_part, preferred_element_type=jnp.float32)
        return mixed.astype(jnp.bfloat16)

    output = lax.map(
        one_group,
        (
            split_heads(rotated, query_rows),
            split_heads(piece[:, 0], key_rows),
            split_heads(piece[:, 1], key_rows),
        ),
    )
    return jnp.moveaxis(output, 0, 1).reshape(query_rows, head_count, head_dim)


def body(queries, keys_values, positions, documents):
    rotated = rotate(queries[0], positions)
    key_share = rotate(keys_values[:, 0], positions)
    share = jnp.stack([key_share, keys_values[:, 1]], axis=1)
    at_start = lax.axis_index("ctx") == 0
    whole = lax.all_gather(share, "section", axis=2, tiled=True)
    earlier, earlier_docs = shifted((whole, documents), "ctx", 1)
    key_docs = jnp.concatenate(
        [jnp.where(at_start, -1, earlier_docs).astype(jnp.int32), documents], axis=0
    )
    window = jnp.concatenate([earlier, whole], axis=0)
    result = attend(rotated, window, key_docs, documents)
    return result[None]


def solution(mesh):
    placed = (P("section", "ctx", None, None), P("ctx", None, "section", None), P("ctx"), P("ctx"))
    return jax.shard_map(
        body, mesh=mesh, in_specs=placed, out_specs=P("section", "ctx", None, None), check_vma=False
    )
```

profile of v0, /device:TPU:2, one launch (start us, length us, event | category | flops | bytes accessed | tf_op | source)
XLA Modules:
  0.0 344.2 jit_solution(13861718311189007667)
XLA Ops:
  6.5 0.0 copy-start
  6.5 0.0 all-gather.2.cloned.1.call-start
  6.5 0.7 convert_element_type.37
  7.2 3.3 fusion.33
  10.5 0.7 copy.20
  11.2 0.1 bitcast_convert_fusion.1
  11.3 0.7 copy.21
  12.0 0.4 multiply_cosine_fusion
  12.4 0.1 fusion.29
  12.5 1.1 pad_maximum_fusion
  13.6 0.0 all-gather.2.cloned.1.call-update
  13.6 109.1 %all-gather.2.cloned.1.call-done = bf16[384,2,40,128]{0,3,2,1:T(8,128)(2,1)} async-done(((bf16[384,2,5,128]{0,3,2,1:T(8,128)(2,1)}), bf16[384,2,40,128]{0,3,2,1:T(8,128)(2,1)}) %all-gather.2.cloned.1.call-update) | async-done | bytes 7864336 | tf_op jit(solution)/shard_map/all_gather | solution.py:75
  122.7 1.9 collective-permute-start
  124.6 0.0 copy-done
  124.6 3.6 %collective-permute-start.1 = (s32[384]{0:T(512)S(1)}, s32[384]{0:T(512)S(1)}, u32[]{:S(2)}, u32[]{:S(2)}) collective-permute-start(s32[384]{0:T(512)S(1)} %copy-done), channel_id=1, source_target_pairs={{0,1},{1,2},{2,3},{3,4},{4,5},{5,6},{6,7},{7,8},{8,9},{9,10},{10,1... | collective-permute-start | bytes 4616 | tf_op jit(solution)/shard_map/ppermute | solution.py:10
  128.2 0.1 copy.14
  128.3 0.1 copy.15
  128.4 2.6 bitcast_convert_fusion
  131.1 2.6 subtract_convert_fusion
  133.7 0.9 copy.16
  134.7 0.9 copy.17
  135.6 4.1 %maximum_bitcast_fusion = bf16[5,384,8,128]{3,1,2,0:T(8,128)(2,1)} fusion(bf16[384,5,8,64]{3,0,2,1:T(8,128)(2,1)S(1)} %bitcast.53, bf16[384,5,8,64]{3,0,2,1:T(8,128)(2,1)S(1)} %bitcast.52), kind=kLoop, calls=%fused_computation.28 | loop fusion | flops 7864320 | bytes 7864320 | tf_op jit(solution)/shard_map/transpose | solution.py:38
  139.7 74.6 %collective-permute-done.1 = s32[384]{0:T(512)S(1)} collective-permute-done((s32[384]{0:T(512)S(1)}, s32[384]{0:T(512)S(1)}, u32[]{:S(2)}, u32[]{:S(2)}) %collective-permute-start.1) | collective-permute-done | bytes 1568 | tf_op jit(solution)/shard_map/ppermute | solution.py:10
  214.2 0.0 slice-start
  214.3 0.0 slice-start.1
  214.3 0.0 collective-permute-done
  214.3 8.1 %constant_dynamic-update-slice_fusion.1 = bf16[768,2,40,128]{0,3,2,1:T(8,128)(2,1)} fusion(bf16[384,2,40,128]{0,3,2,1:T(8,128)(2,1)} %collective-permute-done), kind=kLoop, calls=%fused_computation.39 | loop fusion | bytes 15728640
  222.4 0.0 slice-done
  222.4 0.0 slice-done.1
  222.4 4.3 %constant_dynamic-update-slice_fusion = bf16[768,2,40,128]{0,3,2,1:T(8,128)(2,1)} fusion(bf16[768,2,40,128]{0,3,2,1:T(8,128)(2,1)} %constant_dynamic-update-slice_fusion.1, bf16[384,2,40,128]{0,3,2,1:T(8,128)(2,1)S(1)} %bitcast.55), kind=kLoop, calls=%fused_computation.38 | loop fusion | bytes 15728640 | tf_op jit(solution)/shard_map/concatenate | solution.py:80
  226.7 11.1 %fusion.32 = (bf16[768,1,40,128]{0,3,2,1:T(8,128)(2,1)}, bf16[768,1,40,128]{0,3,2,1:T(8,128)(2,1)}) fusion(bf16[768,2,40,128]{0,3,2,1:T(8,128)(2,1)} %constant_dynamic-update-slice_fusion), kind=kLoop, calls=%fused_computation.45 | loop fusion | bytes 31457280 | tf_op jit(solution)/shard_map/slice | solution.py:63
  237.8 10.6 %copy.18 = bf16[768,5,8,128]{3,0,2,1:T(8,128)(2,1)} copy(bf16[768,5,8,128]{0,3,2,1:T(8,128)(2,1)} %bitcast.51) | data formatting | bytes 15728640 | tf_op jit(solution)/shard_map/reshape;squeeze | solution.py:38
  248.4 82.5 %while.11 = (s32[]{:T(128)}, bf16[5,384,8,128]{1,3,2,0:T(8,128)(2,1)}, bf16[5,768,8,128]{1,3,2,0:T(8,128)(2,1)}, bf16[5,384,8,128]{3,1,2,0:T(8,128)(2,1)}, bf16[...) while((s32[]{:T(128)}, ...), condition=%wide.region_3.4_spmd.clone, body=%wide.region_0.3_spmd.clone.sunk | while | flops 1228112640 | bytes 43090012 | solution.py:59
  248.4 3.0 fusion.44
  251.5 0.4 fusion.45
  251.9 6.5 %fusion.46 = (f32[8,384]{1,0:T(8,128)S(1)}, f32[8,384,768]{2,1,0:T(8,128)}) fusion(f32[8,384,768]{2,1,0:T(8,128)S(1)} %fusion.44, pred[384,768]{1,0:T(8,128)(4,1)S(1)} %fusion.45), kind=kOutput, calls=%fused_computation.44.clone.1 | output fusion | flops 14156543 | bytes 19181568 | tf_op jit(solution)/shard_map/while/body/eval_jaxpr/sub | solution.py:54
  258.3 6.6 %fusion.47 = bf16[5,384,8,128]{1,3,2,0:T(8,128)(2,1)} fusion(bf16[5,384,8,128]{1,3,2,0:T(8,128)(2,1)} %get-tuple-element.150, s32[]{:T(128)} %get-tuple-element.149, f32[8,384,768]{2,1,0:T(8,128)} %get-tuple-element.138, f32[8,384]{1,0:T(8,128)S(1)} %get-tuple-element.139, bf16[5,768,8,128]{1,3,2,0:T(8,128)(2,1)} %get-tuple-element.160), kind=kOutput, calls=%fused_computation.17.clone.1 | convolution fusion | flops 609091584 | bytes 11809792 | tf_op jit(solution)/shard_map/while/body/eval_jaxpr/hqk,khd->qhd/dot_general | solution.py:56
  265.0 3.0 fusion.44
  268.0 0.4 fusion.45
  268.4 6.5 %fusion.46 = (f32[8,384]{1,0:T(8,128)S(1)}, f32[8,384,768]{2,1,0:T(8,128)}) fusion(f32[8,384,768]{2,1,0:T(8,128)S(1)} %fusion.44, pred[384,768]{1,0:T(8,128)(4,1)S(1)} %fusion.45), kind=kOutput, calls=%fused_computation.44.clone.1 | output fusion | flops 14156543 | bytes 19181568 | tf_op jit(solution)/shard_map/while/body/eval_jaxpr/sub | solution.py:54
  274.9 6.6 %fusion.47 = bf16[5,384,8,128]{1,3,2,0:T(8,128)(2,1)} fusion(bf16[5,384,8,128]{1,3,2,0:T(8,128)(2,1)} %get-tuple-element.150, s32[]{:T(128)} %get-tuple-element.149, f32[8,384,768]{2,1,0:T(8,128)} %get-tuple-element.138, f32[8,384]{1,0:T(8,128)S(1)} %get-tuple-element.139, bf16[5,768,8,128]{1,3,2,0:T(8,128)(2,1)} %get-tuple-element.160), kind=kOutput, calls=%fused_computation.17.clone.1 | convolution fusion | flops 609091584 | bytes 11809792 | tf_op jit(solution)/shard_map/while/body/eval_jaxpr/hqk,khd->qhd/dot_general | solution.py:56
  281.5 3.0 fusion.44
  284.5 0.4 fusion.45
  284.9 6.5 %fusion.46 = (f32[8,384]{1,0:T(8,128)S(1)}, f32[8,384,768]{2,1,0:T(8,128)}) fusion(f32[8,384,768]{2,1,0:T(8,128)S(1)} %fusion.44, pred[384,768]{1,0:T(8,128)(4,1)S(1)} %fusion.45), kind=kOutput, calls=%fused_computation.44.clone.1 | output fusion | flops 14156543 | bytes 19181568 | tf_op jit(solution)/shard_map/while/body/eval_jaxpr/sub | solution.py:54
  291.4 6.5 %fusion.47 = bf16[5,384,8,128]{1,3,2,0:T(8,128)(2,1)} fusion(bf16[5,384,8,128]{1,3,2,0:T(8,128)(2,1)} %get-tuple-element.150, s32[]{:T(128)} %get-tuple-element.149, f32[8,384,768]{2,1,0:T(8,128)} %get-tuple-element.138, f32[8,384]{1,0:T(8,128)S(1)} %get-tuple-element.139, bf16[5,768,8,128]{1,3,2,0:T(8,128)(2,1)} %get-tuple-element.160), kind=kOutput, calls=%fused_computation.17.clone.1 | convolution fusion | flops 609091584 | bytes 11809792 | tf_op jit(solution)/shard_map/while/body/eval_jaxpr/hqk,khd->qhd/dot_general | solution.py:56
  297.9 3.0 fusion.44
  301.0 0.4 fusion.45
  301.3 6.5 %fusion.46 = (f32[8,384]{1,0:T(8,128)S(1)}, f32[8,384,768]{2,1,0:T(8,128)}) fusion(f32[8,384,768]{2,1,0:T(8,128)S(1)} %fusion.44, pred[384,768]{1,0:T(8,128)(4,1)S(1)} %fusion.45), kind=kOutput, calls=%fused_computation.44.clone.1 | output fusion | flops 14156543 | bytes 19181568 | tf_op jit(solution)/shard_map/while/body/eval_jaxpr/sub | solution.py:54
  307.8 6.7 %fusion.47 = bf16[5,384,8,128]{1,3,2,0:T(8,128)(2,1)} fusion(bf16[5,384,8,128]{1,3,2,0:T(8,128)(2,1)} %get-tuple-element.150, s32[]{:T(128)} %get-tuple-element.149, f32[8,384,768]{2,1,0:T(8,128)} %get-tuple-element.138, f32[8,384]{1,0:T(8,128)S(1)} %get-tuple-element.139, bf16[5,768,8,128]{1,3,2,0:T(8,128)(2,1)} %get-tuple-element.160), kind=kOutput, calls=%fused_computation.17.clone.1 | convolution fusion | flops 609091584 | bytes 11809792 | tf_op jit(solution)/shard_map/while/body/eval_jaxpr/hqk,khd->qhd/dot_general | solution.py:56
  314.5 3.0 fusion.44
  317.6 0.4 fusion.45
  317.9 6.5 %fusion.46 = (f32[8,384]{1,0:T(8,128)S(1)}, f32[8,384,768]{2,1,0:T(8,128)}) fusion(f32[8,384,768]{2,1,0:T(8,128)S(1)} %fusion.44, pred[384,768]{1,0:T(8,128)(4,1)S(1)} %fusion.45), kind=kOutput, calls=%fused_computation.44.clone.1 | output fusion | flops 14156543 | bytes 19181568 | tf_op jit(solution)/shard_map/while/body/eval_jaxpr/sub | solution.py:54
  324.4 6.6 %fusion.47 = bf16[5,384,8,128]{1,3,2,0:T(8,128)(2,1)} fusion(bf16[5,384,8,128]{1,3,2,0:T(8,128)(2,1)} %get-tuple-element.150, s32[]{:T(128)} %get-tuple-element.149, f32[8,384,768]{2,1,0:T(8,128)} %get-tuple-element.138, f32[8,384]{1,0:T(8,128)S(1)} %get-tuple-element.139, bf16[5,768,8,128]{1,3,2,0:T(8,128)(2,1)} %get-tuple-element.160), kind=kOutput, calls=%fused_computation.17.clone.1 | convolution fusion | flops 609091584 | bytes 11809792 | tf_op jit(solution)/shard_map/while/body/eval_jaxpr/hqk,khd->qhd/dot_general | solution.py:56
  331.0 6.4 %copy.19 = bf16[384,5,8,128]{3,2,1,0:T(8,128)(2,1)} copy(bf16[384,5,8,128]{0,3,2,1:T(8,128)(2,1)} %bitcast.13) | data formatting | bytes 7864320 | tf_op jit(solution)/shard_map/transpose | solution.py:67
  (6 shorter events, 0.0 us)
Async XLA Ops:
  6.5 118.1 %copy-start = (s32[384]{0:T(512)S(1)}, s32[384]{0:T(512)}, u32[]{:S(2)}) copy-start(s32[384]{0:T(512)} %param.9) | copy-start | bytes 4612
  6.5 116.1 %all-gather.2.cloned.1.call-start = ((), (), s32[]{:S(2)}) async-start(), calls=%async_computation | async-start | bytes 8847360 | tf_op jit(solution)/shard_map/all_gather | solution.py:75
  122.7 91.6 %collective-permute-start = (bf16[384,2,40,128]{0,3,2,1:T(8,128)(2,1)}, bf16[384,2,40,128]{0,3,2,1:T(8,128)(2,1)}, u32[]{:S(2)}, u32[]{:S(2)}) collective-permute-start(bf16[384,2,40,128]{0,3,2,1:T(8,128)(2,1)} %all-gather.2.cloned.1.call-done), channel_id=1, source_target_pairs={{0,1},{1,2},{2,3},{3,4},{4,5},{5,6},{6,7},{7,8},{8,9},{9,10},{10,1... | collective-permute-start | bytes 23592968 | tf_op jit(solution)/shard_map/ppermute | solution.py:10
  124.6 89.6 %collective-permute-start.1 = (s32[384]{0:T(512)S(1)}, s32[384]{0:T(512)S(1)}, u32[]{:S(2)}, u32[]{:S(2)}) collective-permute-start(s32[384]{0:T(512)S(1)} %copy-done), channel_id=1, source_target_pairs={{0,1},{1,2},{2,3},{3,4},{4,5},{5,6},{6,7},{7,8},{8,9},{9,10},{10,1... | collective-permute-start | bytes 4616 | tf_op jit(solution)/shard_map/ppermute | solution.py:10
  214.2 8.1 %slice-start = ((s8[7864320]{0:T(1024)(128)(4,1)}), s8[4194304]{0:T(1024)(128)(4,1)S(1)}, s32[]{:S(2)}) async-start(s8[7864320]{0:T(1024)(128)(4,1)} %bitcast.54), calls=%async_computation.1 | async-start | bytes 8388608
  214.3 8.1 %slice-start.1 = ((s8[7864320]{0:T(1024)(128)(4,1)}), s8[3670016]{0:T(1024)(128)(4,1)S(1)}, s32[]{:S(2)}) async-start(s8[7864320]{0:T(1024)(128)(4,1)} %bitcast.54), calls=%async_computation.2 | async-start | bytes 7340032
Sparse Core Ops, SparseCore 0:
  13.7 108.9 all-gather.1
where the time goes:
time: 345 us; the launch traced here: 344 us
  waiting for transfers between devices  184 us (53%)
  matrix products  48.2 us (14%)
  local copies, waits for them, and re-layouts  47.3 us (14%)
  other arithmetic  46 us (13%)
  between operations  13.5 us (4%)
  starting transfers between devices  5.48 us (2%)
    all_gather x1, waiting for transfers between devices, body(): whole = lax.all_gather(share, 'section', axis=2, tiled=True)  109 us
    ppermute x2, waiting for transfers between devices, shifted(): return lax.ppermute(block, axis, route)  74.6 us
    dot_general x5, matrix products, one_group(): jnp.einsum('hqk,khd->qhd', probs, value_part, preferred_element_type=jnp....  33 us
    sub x5, other arithmetic, one_group(): weights = jnp.exp(scores - largest)  32.5 us
    dot_general x5, matrix products, one_group(): jnp.einsum('qhd,khd->hqk', query_part, key_part, preferred_element_type=j...  15.2 us
    slice x1, local copies, waits for them, and re-layouts, attend(): piece[:, 0]  11.1 us
    another operation x1, local copies, waits for them, and re-layouts, split_heads(): return jnp.moveaxis(values.reshape(length, groups, factor, head_dim), 1, 0)  10.6 us
    unnamed x9, local copies, waits for them, and re-layouts  9.43 us
  transfers between devices with their start and end apart: 3, of which 2 were waited for; matrix products, arithmetic and copies ran while one was open for 3% of the time, Pallas kernels for 0%

commit v1 on v0

--- a/solution.py
+++ b/solution.py
@@ -72,7 +72,9 @@
     key_share = rotate(keys_values[:, 0], positions)
     share = jnp.stack([key_share, keys_values[:, 1]], axis=1)
     at_start = lax.axis_index("ctx") == 0
-    whole = lax.all_gather(share, "section", axis=2, tiled=True)
+    whole = jnp.concatenate(
+        lax.all_to_all(jnp.stack([share] * lax.axis_size("section")), "section", 0, 0), axis=2
+    )
     earlier, earlier_docs = shifted((whole, documents), "ctx", 1)
     key_docs = jnp.concatenate(
         [jnp.where(at_start, -1, earlier_docs).astype(jnp.int32), documents], axis=0

time: 345 us -> 313 us (0.907)
  waiting for transfers between devices: 184 us -> 74 us
  blocking collectives: 0 us -> 97.3 us
  local copies, waits for them, and re-layouts: 47.3 us -> 30.4 us
  between operations: 13.5 us -> 0.15 us
  other arithmetic: 46 us -> 56.1 us
    all_gather x1 -> x0, waiting for transfers between devices: 109 us -> none  [body(): whole = lax.all_gather(share, 'section', axis=2, tiled=True)]
    all_to_all x0 -> x1, blocking collectives: none -> 97.3 us  [body(): lax.all_to_all(jnp.stack([share] * lax.axis_size('section')), 'section',...]
    slice x1 -> x0, local copies, waits for them, and re-layouts: 11.1 us -> none  [attend(): piece[:, 0]]
    concatenate x0 -> x1, other arithmetic: none -> 11.1 us  [body(): window = jnp.concatenate([earlier, whole], axis=0)]
    unnamed x9 -> x4, local copies, waits for them, and re-layouts: 9.43 us -> 1.34 us
    concatenate x1 -> x0, local copies, waits for them, and re-layouts: 4.32 us -> none  [body(): window = jnp.concatenate([earlier, whole], axis=0)]
    all_to_all x0 -> x1, local copies, waits for them, and re-layouts: none -> 4.11 us  [body(): lax.all_to_all(jnp.stack([share] * lax.axis_size('section')), 'section',...]
  transfers between devices with their start and end apart: 3 -> 2, of which waited for: 2 -> 1; matrix products, arithmetic and copies ran while one was open for 3% -> 4% of each run, Pallas kernels for 0% -> 0%
where the time goes in v1:
time: 313 us; the launch traced here: 312 us
  blocking collectives  97.3 us (31%)
  waiting for transfers between devices  74 us (24%)
  other arithmetic  56.1 us (18%)
  matrix products  47.9 us (15%)
  local copies, waits for them, and re-layouts  30.4 us (10%)
  starting transfers between devices  6.02 us (2%)
    all_to_all x1, blocking collectives, body(): lax.all_to_all(jnp.stack([share] * lax.axis_size('section')), 'section',...  97.3 us
    ppermute x2, waiting for transfers between devices, shifted(): return lax.ppermute(block, axis, route)  74 us
    dot_general x5, matrix products, one_group(): jnp.einsum('hqk,khd->qhd', probs, value_part, preferred_element_type=jnp....  32.7 us
    sub x5, other arithmetic, one_group(): weights = jnp.exp(scores - largest)  32.5 us
    dot_general x5, matrix products, one_group(): jnp.einsum('qhd,khd->hqk', query_part, key_part, preferred_element_type=j...  15.2 us
    concatenate x1, other arithmetic, body(): window = jnp.concatenate([earlier, whole], axis=0)  11.1 us
    another operation x1, local copies, waits for them, and re-layouts, split_heads(): return jnp.moveaxis(values.reshape(length, groups, factor, head_dim), 1, 0)  10.6 us
    transpose x1, local copies, waits for them, and re-layouts, attend(): return jnp.moveaxis(output, 0, 1).reshape(query_rows, head_count, head_dim)  6.36 us
  transfers between devices with their start and end apart: 2, of which 1 were waited for; matrix products, arithmetic and copies ran while one was open for 4% of the time, Pallas kernels for 0%

profile of v1, /device:TPU:2, one launch (start us, length us, event | category | flops | bytes accessed | tf_op | source)
XLA Modules:
  0.0 312.0 jit_solution(1934835401298501805)
XLA Ops:
  0.0 0.7 convert_element_type.37
  0.7 3.2 %fusion.33 = (bf16[384,1,5,128]{3,1,2,0:T(2,128)(2,1)S(1)}, bf16[384,1,5,128]{3,1,2,0:T(2,128)(2,1)S(1)}) fusion(bf16[384,2,5,128]{3,1,2,0:T(2,128)(2,1)} %param.7), kind=kLoop, calls=%fused_computation.47 | loop fusion | bytes 1966080 | tf_op jit(solution)/shard_map/slice | solution.py:72
  3.9 0.7 copy.40
  4.6 0.1 bitcast_convert_fusion.1
  4.7 0.7 copy.41
  5.3 0.4 multiply_cosine_fusion
  5.8 0.1 fusion.30
  5.9 0.1 pad_maximum_fusion.1
  6.0 0.7 copy.32
  6.7 1.9 stack.5
  8.6 97.3 %all_to_all.5 = bf16[8,384,2,5,128]{4,1,3,2,0:T(8,128)(2,1)S(1)} all-to-all(bf16[8,384,2,5,128]{4,1,3,2,0:T(8,128)(2,1)S(1)} %stack.5), channel_id=1, replica_groups=mesh['section'=8,'ctx'=32] {'section'}, dimensions={0} | all-to-all | bytes 15728640 | tf_op jit(solution)/shard_map/all_to_all | solution.py:76
  105.9 0.0 copy-start
  105.9 4.1 %copy.33 = bf16[8,384,2,5,128]{4,1,3,0,2:T(8,128)(2,1)} copy(bf16[8,384,2,5,128]{4,1,3,2,0:T(8,128)(2,1)S(1)} %all_to_all.5) | data formatting | bytes 15728640 | tf_op jit(solution)/shard_map/all_to_all | solution.py:76
  110.0 1.9 collective-permute-start
  111.9 0.0 copy-done
  111.9 4.1 %collective-permute-start.1 = (s32[384]{0:T(512)S(1)}, s32[384]{0:T(512)S(1)}, u32[]{:S(2)}, u32[]{:S(2)}) collective-permute-start(s32[384]{0:T(512)S(1)} %copy-done), channel_id=1, source_target_pairs={{0,1},{1,2},{2,3},{3,4},{4,5},{5,6},{6,7},{7,8},{8,9},{9,10},{10,1... | collective-permute-start | bytes 4616 | tf_op jit(solution)/shard_map/ppermute | solution.py:10
  116.1 0.1 copy.35
  116.2 0.1 copy.36
  116.3 2.6 bitcast_convert_fusion
  119.0 2.6 subtract_convert_fusion
  121.6 0.9 copy.37
  122.5 0.9 copy.38
  123.5 4.1 %maximum_bitcast_fusion = bf16[5,384,8,128]{3,1,2,0:T(8,128)(2,1)} fusion(bf16[384,5,8,64]{3,0,2,1:T(8,128)(2,1)S(1)} %bitcast.58, bf16[384,5,8,64]{3,0,2,1:T(8,128)(2,1)S(1)} %bitcast.57), kind=kLoop, calls=%fused_computation.32 | loop fusion | flops 7864320 | bytes 7864320 | tf_op jit(solution)/shard_map/transpose | solution.py:38
  127.6 74.0 %collective-permute-done.1 = s32[384]{0:T(512)S(1)} collective-permute-done((s32[384]{0:T(512)S(1)}, s32[384]{0:T(512)S(1)}, u32[]{:S(2)}, u32[]{:S(2)}) %collective-permute-start.1) | collective-permute-done | bytes 1568 | tf_op jit(solution)/shard_map/ppermute | solution.py:10
  201.6 0.0 collective-permute-done
  201.6 11.1 %pad_maximum_fusion = (bf16[768,1,40,128]{3,0,2,1:T(8,128)(2,1)}, bf16[768,1,40,128]{3,0,2,1:T(8,128)(2,1)}) fusion(bf16[384,2,40,128]{3,0,2,1:T(8,128)(2,1)} %bitcast.55, bf16[384,2,40,128]{3,0,2,1:T(8,128)(2,1)} %collective-permute-done), kind=kLoop, calls=%fused_computation.29 | loop fusion | flops 31457280 | bytes 31457280 | tf_op jit(solution)/shard_map/concatenate | solution.py:82
  212.7 10.6 %copy.34 = bf16[768,5,8,128]{0,3,2,1:T(8,128)(2,1)} copy(bf16[768,5,8,128]{3,0,2,1:T(8,128)(2,1)} %bitcast.56) | data formatting | bytes 15728640 | tf_op jit(solution)/shard_map/reshape;squeeze | solution.py:38
  223.3 82.3 %while.11 = (s32[]{:T(128)}, bf16[5,384,8,128]{1,3,2,0:T(8,128)(2,1)}, bf16[5,768,8,128]{1,3,2,0:T(8,128)(2,1)}, bf16[5,384,8,128]{3,1,2,0:T(8,128)(2,1)}, bf16[...) while((s32[]{:T(128)}, ...), condition=%wide.region_3.4_spmd.clone, body=%wide.region_0.3_spmd.clone.sunk | while | flops 1228112640 | bytes 43090012 | solution.py:59
  223.3 3.0 fusion.44
  226.4 0.4 fusion.45
  226.7 6.5 %fusion.46 = (f32[8,384]{1,0:T(8,128)S(1)}, f32[8,384,768]{2,1,0:T(8,128)}) fusion(f32[8,384,768]{2,1,0:T(8,128)S(1)} %fusion.44, pred[384,768]{1,0:T(8,128)(4,1)S(1)} %fusion.45), kind=kOutput, calls=%fused_computation.46.clone.1 | output fusion | flops 14156543 | bytes 19181568 | tf_op jit(solution)/shard_map/while/body/eval_jaxpr/sub | solution.py:54
  233.2 6.5 %fusion.47 = bf16[5,384,8,128]{1,3,2,0:T(8,128)(2,1)} fusion(bf16[5,384,8,128]{1,3,2,0:T(8,128)(2,1)} %get-tuple-element.150, s32[]{:T(128)} %get-tuple-element.149, f32[8,384,768]{2,1,0:T(8,128)} %get-tuple-element.138, f32[8,384]{1,0:T(8,128)S(1)} %get-tuple-element.139, bf16[5,768,8,128]{1,3,2,0:T(8,128)(2,1)} %get-tuple-element.160), kind=kOutput, calls=%fused_computation.17.clone.1 | convolution fusion | flops 609091584 | bytes 11809792 | tf_op jit(solution)/shard_map/while/body/eval_jaxpr/hqk,khd->qhd/dot_general | solution.py:56
  239.8 3.0 fusion.44
  242.8 0.4 fusion.45
  243.2 6.5 %fusion.46 = (f32[8,384]{1,0:T(8,128)S(1)}, f32[8,384,768]{2,1,0:T(8,128)}) fusion(f32[8,384,768]{2,1,0:T(8,128)S(1)} %fusion.44, pred[384,768]{1,0:T(8,128)(4,1)S(1)} %fusion.45), kind=kOutput, calls=%fused_computation.46.clone.1 | output fusion | flops 14156543 | bytes 19181568 | tf_op jit(solution)/shard_map/while/body/eval_jaxpr/sub | solution.py:54
  249.7 6.6 %fusion.47 = bf16[5,384,8,128]{1,3,2,0:T(8,128)(2,1)} fusion(bf16[5,384,8,128]{1,3,2,0:T(8,128)(2,1)} %get-tuple-element.150, s32[]{:T(128)} %get-tuple-element.149, f32[8,384,768]{2,1,0:T(8,128)} %get-tuple-element.138, f32[8,384]{1,0:T(8,128)S(1)} %get-tuple-element.139, bf16[5,768,8,128]{1,3,2,0:T(8,128)(2,1)} %get-tuple-element.160), kind=kOutput, calls=%fused_computation.17.clone.1 | convolution fusion | flops 609091584 | bytes 11809792 | tf_op jit(solution)/shard_map/while/body/eval_jaxpr/hqk,khd->qhd/dot_general | solution.py:56
  256.2 3.0 fusion.44
  259.3 0.4 fusion.45
  259.6 6.5 %fusion.46 = (f32[8,384]{1,0:T(8,128)S(1)}, f32[8,384,768]{2,1,0:T(8,128)}) fusion(f32[8,384,768]{2,1,0:T(8,128)S(1)} %fusion.44, pred[384,768]{1,0:T(8,128)(4,1)S(1)} %fusion.45), kind=kOutput, calls=%fused_computation.46.clone.1 | output fusion | flops 14156543 | bytes 19181568 | tf_op jit(solution)/shard_map/while/body/eval_jaxpr/sub | solution.py:54
  266.2 6.6 %fusion.47 = bf16[5,384,8,128]{1,3,2,0:T(8,128)(2,1)} fusion(bf16[5,384,8,128]{1,3,2,0:T(8,128)(2,1)} %get-tuple-element.150, s32[]{:T(128)} %get-tuple-element.149, f32[8,384,768]{2,1,0:T(8,128)} %get-tuple-element.138, f32[8,384]{1,0:T(8,128)S(1)} %get-tuple-element.139, bf16[5,768,8,128]{1,3,2,0:T(8,128)(2,1)} %get-tuple-element.160), kind=kOutput, calls=%fused_computation.17.clone.1 | convolution fusion | flops 609091584 | bytes 11809792 | tf_op jit(solution)/shard_map/while/body/eval_jaxpr/hqk,khd->qhd/dot_general | solution.py:56
  272.7 3.0 fusion.44
  275.8 0.4 fusion.45
  276.1 6.5 %fusion.46 = (f32[8,384]{1,0:T(8,128)S(1)}, f32[8,384,768]{2,1,0:T(8,128)}) fusion(f32[8,384,768]{2,1,0:T(8,128)S(1)} %fusion.44, pred[384,768]{1,0:T(8,128)(4,1)S(1)} %fusion.45), kind=kOutput, calls=%fused_computation.46.clone.1 | output fusion | flops 14156543 | bytes 19181568 | tf_op jit(solution)/shard_map/while/body/eval_jaxpr/sub | solution.py:54
  282.6 6.5 %fusion.47 = bf16[5,384,8,128]{1,3,2,0:T(8,128)(2,1)} fusion(bf16[5,384,8,128]{1,3,2,0:T(8,128)(2,1)} %get-tuple-element.150, s32[]{:T(128)} %get-tuple-element.149, f32[8,384,768]{2,1,0:T(8,128)} %get-tuple-element.138, f32[8,384]{1,0:T(8,128)S(1)} %get-tuple-element.139, bf16[5,768,8,128]{1,3,2,0:T(8,128)(2,1)} %get-tuple-element.160), kind=kOutput, calls=%fused_computation.17.clone.1 | convolution fusion | flops 609091584 | bytes 11809792 | tf_op jit(solution)/shard_map/while/body/eval_jaxpr/hqk,khd->qhd/dot_general | solution.py:56
  289.2 3.0 fusion.44
  292.2 0.4 fusion.45
  292.6 6.5 %fusion.46 = (f32[8,384]{1,0:T(8,128)S(1)}, f32[8,384,768]{2,1,0:T(8,128)}) fusion(f32[8,384,768]{2,1,0:T(8,128)S(1)} %fusion.44, pred[384,768]{1,0:T(8,128)(4,1)S(1)} %fusion.45), kind=kOutput, calls=%fused_computation.46.clone.1 | output fusion | flops 14156543 | bytes 19181568 | tf_op jit(solution)/shard_map/while/body/eval_jaxpr/sub | solution.py:54
  299.1 6.5 %fusion.47 = bf16[5,384,8,128]{1,3,2,0:T(8,128)(2,1)} fusion(bf16[5,384,8,128]{1,3,2,0:T(8,128)(2,1)} %get-tuple-element.150, s32[]{:T(128)} %get-tuple-element.149, f32[8,384,768]{2,1,0:T(8,128)} %get-tuple-element.138, f32[8,384]{1,0:T(8,128)S(1)} %get-tuple-element.139, bf16[5,768,8,128]{1,3,2,0:T(8,128)(2,1)} %get-tuple-element.160), kind=kOutput, calls=%fused_computation.17.clone.1 | convolution fusion | flops 609091584 | bytes 11809792 | tf_op jit(solution)/shard_map/while/body/eval_jaxpr/hqk,khd->qhd/dot_general | solution.py:56
  305.6 6.4 %copy.39 = bf16[384,5,8,128]{3,2,1,0:T(8,128)(2,1)} copy(bf16[384,5,8,128]{0,3,2,1:T(8,128)(2,1)} %bitcast.15) | data formatting | bytes 7864320 | tf_op jit(solution)/shard_map/transpose | solution.py:67
  (5 shorter events, 0.0 us)
Async XLA Ops:
  105.9 6.0 %copy-start = (s32[384]{0:T(512)S(1)}, s32[384]{0:T(512)}, u32[]{:S(2)}) copy-start(s32[384]{0:T(512)} %param.9) | copy-start | bytes 4612
  110.0 91.6 %collective-permute-start = (bf16[384,2,40,128]{3,0,2,1:T(8,128)(2,1)}, bf16[384,2,40,128]{3,0,2,1:T(8,128)(2,1)}, u32[]{:S(2)}, u32[]{:S(2)}) collective-permute-start(bf16[384,2,40,128]{3,0,2,1:T(8,128)(2,1)} %bitcast.54), channel_id=1, source_target_pairs={{0,1},{1,2},{2,3},{3,4},{4,5},{5,6},{6,7},{7,8},{8,9},{9,10},{10,1... | collective-permute-start | bytes 23592968 | tf_op jit(solution)/shard_map/ppermute | solution.py:10
  111.9 89.6 %collective-permute-start.1 = (s32[384]{0:T(512)S(1)}, s32[384]{0:T(512)S(1)}, u32[]{:S(2)}, u32[]{:S(2)}) collective-permute-start(s32[384]{0:T(512)S(1)} %copy-done), channel_id=1, source_target_pairs={{0,1},{1,2},{2,3},{3,4},{4,5},{5,6},{6,7},{7,8},{8,9},{9,10},{10,1... | collective-permute-start | bytes 4616 | tf_op jit(solution)/shard_map/ppermute | solution.py:10
